TPU v7x, 128 devices: a whole 4x4x4 slice. The times are simulated.
128 devices in a mesh: sec: 4 (over y), dev: 32 (over z, x, core).
Axes of the slice: x: 4, y: 4, z: 4, core: 2. Of those that a mesh axis runs over, the one named last changes fastest.
Arguments:
- hidden: bfloat16 [2048, 3584], P(('sec', 'dev')), may hold values from -6 to 6
- expert_ids: int32 [2048, 8], P(('sec', 'dev')), may hold values from 0 to 127, all different within a row; in each aligned block of 16 rows (0 to 15, 16 to 31, ...) at most 2 rows name the same one
- route_weights: float32 [2048, 8], P(('sec', 'dev')), may hold values from 0.1 to 1
- w_gate_up: bfloat16 [128, 3584, 2048], P(('sec', 'dev')), may hold values from -0.09375 to 0.09375
- w_down: bfloat16 [128, 1024, 3584], P(('sec', 'dev')), may hold values from -0.1875 to 0.1875
- query_latent: bfloat16 [512, 128, 512], P(('sec', 'dev')), may hold values from -400 to 400
- query_rope: bfloat16 [512, 64, 128], P(('sec', 'dev')), may hold values from -6 to 6
- latent_cache: bfloat16 [512, 512, 512], P(('sec', 'dev')), may hold values from -4 to 4
- rope_cache: bfloat16 [512, 64, 512], P(('sec', 'dev')), may hold values from -6 to 6
- cache_lengths: int32 [512], P(('sec', 'dev')), may hold values from 64 to 512
Outputs:
- moe_out: bfloat16 [2048, 3584], P(('sec', 'dev'))
- expert_load: float32 [128], replicated
- attention_out: bfloat16 [512, 128, 512], P(('sec', 'dev'))
Inputs may be any that keep to these rules, and one draw needn't show every extreme that they name: `expert_ids`: in the rows of one device no expert is named more than 2 times; in some device's rows some expert is named exactly 2 times.
All inputs are finite; a program needn't handle non-finite values.
Results may differ from a plain program's by a relative error of at most 0.008.
Values may be sent and summed in bfloat16 or wider, within the bound.
No kernel may reach another device: no remote copies, remote signals or barrier semaphores. Data moves between devices by JAX's collectives and lax.ppermute only.
A program may use at most 128 MiB of HBM per device.

v0:
```python
import jax
import jax.numpy as jnp
from jax import lax
from jax.sharding import PartitionSpec as P


def attend(query_latent, query_rope, latent_cache, rope_cache, cache_lengths):
    factor = (query_latent.shape[2] + query_rope.shape[1]) ** (-0.5)
    scores = jnp.einsum(
        "rhc,rtc->rht", query_latent, latent_cache, preferred_element_type=jnp.float32
    )
    scores = scores + jnp.einsum(
        "rph,rpt->rht", query_rope, rope_cache, preferred_element_type=jnp.float32
    )
    scores = scores * factor
    positions = jnp.arange(latent_cache.shape[1], dtype=jnp.int32)
    live_mask = positions[None, None, :] < cache_lengths[:, None, None]
    scores = jnp.where(live_mask, scores, -1e30)
    highest = jnp.max(scores, axis=-1, keepdims=True)
    powers = jnp.exp(scores - highest)
    attention_weights = (powers / jnp.sum(powers, axis=-1, keepdims=True)).astype(jnp.bfloat16)
    result = jnp.einsum(
        "rht,rtc->rhc", attention_weights, latent_cache, preferred_element_type=jnp.float32
    )
    return result.astype(jnp.bfloat16)


def expert_apply(received, w_gate_up, w_down):
    shape_in = received.shape
    flat_rows = received.reshape(-1, shape_in[-1])
    projected = jnp.dot(flat_rows, w_gate_up[0], preferred_element_type=jnp.float32)
    hidden_units = w_down.shape[1]
    activated = (jax.nn.silu(projected[:, :hidden_units]) * projected[:, hidden_units:]).astype(
        jnp.bfloat16
    )
    produced = jnp.dot(activated, w_down[0], preferred_element_type=jnp.float32).astype(
        jnp.bfloat16
    )
    return produced.reshape(shape_in)


def per_device(
    hidden,
    expert_ids,
    route_weights,
    w_gate_up,
    w_down,
    query_latent,
    query_rope,
    latent_cache,
    rope_cache,
    cache_lengths,
):
    row_count, model_width = hidden.shape
    top_count = expert_ids.shape[1]
    sections = lax.axis_size("sec")
    members = lax.axis_size("dev")
    experts = sections * members
    capacity = 2 * row_count * top_count // experts
    flat_ids = expert_ids.reshape(-1)
    expert_range = jnp.arange(experts, dtype=jnp.int32)
    onehot = (flat_ids[:, None] == expert_range[None, :]).astype(jnp.int32)
    earlier = jnp.cumsum(onehot, axis=0) - onehot
    rank_in = jnp.sum(earlier * onehot, axis=1)
    slot_index = flat_ids * capacity + rank_in
    slot_range = jnp.arange(experts * capacity, dtype=jnp.int32)
    placer = (slot_range[:, None] == slot_index[None, :]).reshape(
        experts * capacity, row_count, top_count
    )
    placer = jnp.sum(placer.astype(jnp.int32), axis=2).astype(jnp.bfloat16)
    outgoing = jnp.dot(placer, hidden, preferred_element_type=jnp.float32).astype(jnp.bfloat16)
    outgoing = outgoing.reshape(experts, capacity, model_width)
    counts = jnp.sum(onehot, axis=0).astype(jnp.float32)
    totals = lax.psum(counts, ("sec", "dev"))
    expert_load = totals / float(row_count * top_count)
    returned = lax.all_to_all(
        expert_apply(
            lax.all_to_all(outgoing, ("sec", "dev"), split_axis=0, concat_axis=0, tiled=True),
            w_gate_up,
            w_down,
        ),
        ("sec", "dev"),
        split_axis=0,
        concat_axis=0,
        tiled=True,
    )
    picked = returned.reshape(experts * capacity, model_width)[slot_index]
    picked = picked.reshape(row_count, top_count, model_width)
    moe_out = jnp.einsum("rk,rkd->rd", route_weights, picked.astype(jnp.float32)).astype(
        jnp.bfloat16
    )
    attention_out = attend(query_latent, query_rope, latent_cache, rope_cache, cache_lengths)
    return (moe_out, expert_load, attention_out)


def solution(mesh):
    return jax.shard_map(
        per_device,
        mesh=mesh,
        in_specs=(
            P(("sec", "dev"), None),
            P(("sec", "dev"), None),
            P(("sec", "dev"), None),
            P(("sec", "dev"), None, None),
            P(("sec", "dev"), None, None),
            P(("sec", "dev"), None, None),
            P(("sec", "dev"), None, None),
            P(("sec", "dev"), None, None),
            P(("sec", "dev"), None, None),
            P(("sec", "dev")),
        ),
        out_specs=(P(("sec", "dev"), None), P(), P(("sec", "dev"), None, None)),
        check_vma=False,
    )
```

profile of v0, /device:TPU:1, one launch (start us, length us, event | category | flops | bytes accessed | tf_op | source)
XLA Modules:
  0.0 167.7 jit_solution(17703179839657976555)
XLA Ops:
  0.6 0.0 copy-start
  0.6 0.9 copy.17
  1.6 0.1 eq.30
  1.6 0.1 fusion.18
  1.7 0.2 reduce_window_sum.11
  1.9 0.2 fusion.19
  2.1 0.1 reduce_sum.41
  2.2 0.1 convert_reduce_fusion
  2.3 2.8 %convolution_convert_fusion = bf16[256,3584]{1,0:T(8,128)(2,1)} fusion(bf16[16,3584]{1,0:T(8,128)(2,1)} %param.10, s32[256,16]{0,1:T(8,128)S(1)} %convert_reduce_fusion), kind=kOutput, calls=%fused_computation.7 | convolution fusion | flops 30281728 | bytes 1966080 | tf_op jit(solution)/shard_map/dot_general | solution.py:71
  5.1 4.7 %reshape.91 = bf16[128,2,3584]{2,1,0:T(2,128)(2,1)} reshape(bf16[256,3584]{1,0:T(8,128)(2,1)} %convolution_convert_fusion) | data formatting | bytes 3670016 | tf_op jit(solution)/shard_map/reshape | solution.py:72
  9.9 0.0 copy-start.4
  9.9 11.9 %all-to-all-start = ((bf16[128,2,3584]{2,1,0:T(2,128)(2,1)}), bf16[128,2,3584]{2,1,0:T(2,128)(2,1)}, u32[]{:S(2)}, u32[]{:S(2)}) async-start(bf16[128,2,3584]{2,1,0:T(2,128)(2,1)} %reshape.91), calls=%async_computation | async-start | bytes 3670016 | tf_op jit(solution)/shard_map/all_to_all | solution.py:78
  21.8 0.1 mul.41
  21.9 0.0 copy-done.4
  21.9 0.1 copy.19
  22.0 78.6 %psum.7 = f32[128]{0:T(128)S(1)} all-reduce(f32[128]{0:T(128)S(1)} %convert_element_type.38), channel_id=1, replica_groups=mesh['sec'=4,'dev'=32] {'sec','dev'}, use_global_device_ids=true, to_apply=%region_4.5 | all-reduce | flops 128 | bytes 1024 | tf_op jit(solution)/shard_map/psum | solution.py:74
  100.5 0.0 all-to-all-done
  100.5 4.9 %reshape.92 = bf16[256,3584]{1,0:T(8,128)(2,1)} reshape(bf16[128,2,3584]{2,1,0:T(2,128)(2,1)} %all-to-all-done) | data formatting | bytes 3670016 | tf_op jit(solution)/shard_map/reshape | solution.py:30
  105.4 7.8 %fusion.1 = f32[256,2048]{1,0:T(8,128)S(1)} fusion(bf16[256,3584]{1,0:T(8,128)(2,1)} %reshape.92, bf16[1,3584,2048]{2,1,0:T(8,128)(2,1)} %param.13), kind=kOutput, calls=%fused_computation.2 | convolution fusion | flops 3758096384 | bytes 18612224 | tf_op jit(solution)/shard_map/dot_general | solution.py:31
  113.2 6.4 %fusion.5 = bf16[256,3584]{1,0:T(8,128)(2,1)} fusion(bf16[1,1024,3584]{2,1,0:T(8,128)(2,1)} %param.14, f32[256,2048]{1,0:T(8,128)S(1)} %fusion.1), kind=kOutput, calls=%fused_computation.6 | convolution fusion | flops 1881538560 | bytes 11272192 | tf_op jit(solution)/shard_map/dot_general | solution.py:36
  119.7 4.7 %reshape.93 = bf16[128,2,3584]{2,1,0:T(2,128)(2,1)} reshape(bf16[256,3584]{1,0:T(8,128)(2,1)} %fusion.5) | data formatting | bytes 3670016 | tf_op jit(solution)/shard_map/reshape | solution.py:39
  124.4 0.0 copy-start.5
  124.4 0.0 copy-start.1
  124.4 6.2 %all-to-all-start.1 = ((bf16[128,2,3584]{2,1,0:T(2,128)(2,1)}), bf16[128,2,3584]{2,1,0:T(2,128)(2,1)}, u32[]{:S(2)}, u32[]{:S(2)}) async-start(bf16[128,2,3584]{2,1,0:T(2,128)(2,1)} %reshape.93), calls=%async_computation.1 | async-start | bytes 3670016 | tf_op jit(solution)/shard_map/all_to_all | solution.py:76
  130.7 0.0 copy-start.2
  130.7 0.0 copy-start.3
  130.7 0.0 copy-done.5
  130.7 0.1 iota_compare_fusion.2
  130.8 0.0 copy-done
  130.8 0.0 copy-done.1
  130.8 0.8 fusion.26
  131.6 0.0 copy-done.2
  131.6 0.0 copy-done.3
  131.6 0.4 fusion.11
  132.0 0.3 fusion.25
  132.3 0.5 broadcast_multiply_fusion.1
  132.8 1.8 %convolution_convert_fusion.1 = bf16[4,128,512]{2,1,0:T(8,128)(2,1)} fusion(bf16[4,512,512]{2,1,0:T(8,128)(2,1)S(1)} %copy-done, f32[4,128]{1,0:T(4,128)S(1)} %fusion.25, f32[4,128,512]{2,1,0:T(8,128)S(1)} %fusion.11), kind=kOutput, calls=%fused_computation.13 | convolution fusion | flops 269485056 | bytes 3672064 | tf_op jit(solution)/shard_map/rht,rtc->rhc/dot_general | solution.py:22
  134.7 23.3 %all-to-all-done.1 = bf16[128,2,3584]{2,1,0:T(2,128)(2,1)} async-done(((bf16[128,2,3584]{2,1,0:T(2,128)(2,1)}), bf16[128,2,3584]{2,1,0:T(2,128)(2,1)}, u32[]{:S(2)}, u32[]{:S(2)}) %all-to-all-start.1) | async-done | bytes 1835040 | tf_op jit(solution)/shard_map/all_to_all | solution.py:76
  158.0 4.9 %reshape.94 = bf16[256,3584]{1,0:T(8,128)(2,1)} reshape(bf16[128,2,3584]{2,1,0:T(2,128)(2,1)} %all-to-all-done.1) | data formatting | bytes 3670016 | tf_op jit(solution)/shard_map/reshape | solution.py:87
  162.9 3.8 %gather_fusion = bf16[128,3584]{1,0:T(8,128)(2,1)S(1)} fusion(bf16[256,3584]{1,0:T(8,128)(2,1)} %reshape.94, s32[1024]{0:T(1024)S(1)} %pad_clamp_fusion), kind=kCustom, calls=%fused_computation | custom fusion | bytes 1835520 | tf_op jit(solution)/shard_map/gather | solution.py:87
  166.7 0.4 fusion.13
  167.1 0.7 copy.22
  (4 shorter events, 0.0 us)
Async XLA Ops:
  0.6 130.2 %copy-start = (bf16[4,512,512]{2,1,0:T(8,128)(2,1)S(1)}, bf16[4,512,512]{2,1,0:T(8,128)(2,1)}, u32[]{:S(2)}) copy-start(bf16[4,512,512]{2,1,0:T(8,128)(2,1)} %param.17) | copy-start | bytes 6291460
  9.9 12.0 %copy-start.4 = (f32[16,8]{0,1:T(8,128)S(1)}, f32[16,8]{0,1:T(8,128)}, u32[]{:S(2)}) copy-start(f32[16,8]{0,1:T(8,128)} %param.12) | copy-start | bytes 1540
  9.9 90.6 %all-to-all-start = ((bf16[128,2,3584]{2,1,0:T(2,128)(2,1)}), bf16[128,2,3584]{2,1,0:T(2,128)(2,1)}, u32[]{:S(2)}, u32[]{:S(2)}) async-start(bf16[128,2,3584]{2,1,0:T(2,128)(2,1)} %reshape.91), calls=%async_computation | async-start | bytes 3670016 | tf_op jit(solution)/shard_map/all_to_all | solution.py:78
  124.4 6.3 %copy-start.5 = (s32[4]{0:T(128)S(1)}, s32[4]{0:T(128)}, u32[]{:S(2)}) copy-start(s32[4]{0:T(128)} %param.19) | copy-start | bytes 52
  124.4 6.4 %copy-start.1 = (bf16[4,128,512]{2,1,0:T(8,128)(2,1)S(1)}, bf16[4,128,512]{2,1,0:T(8,128)(2,1)}, u32[]{:S(2)}) copy-start(bf16[4,128,512]{2,1,0:T(8,128)(2,1)} %param.15) | copy-start | bytes 1572868
  124.4 33.6 %all-to-all-start.1 = ((bf16[128,2,3584]{2,1,0:T(2,128)(2,1)}), bf16[128,2,3584]{2,1,0:T(2,128)(2,1)}, u32[]{:S(2)}, u32[]{:S(2)}) async-start(bf16[128,2,3584]{2,1,0:T(2,128)(2,1)} %reshape.93), calls=%async_computation.1 | async-start | bytes 3670016 | tf_op jit(solution)/shard_map/all_to_all | solution.py:76
  130.7 1.0 copy-start.2
  130.7 1.0 copy-start.3
where the time goes:
time: 168 us
  blocking collectives  78.6 us (47%)
  local copies, waits for them, and re-layouts  25 us (15%)
  waiting for transfers between devices  23.3 us (14%)
  matrix products  20.4 us (12%)
  starting transfers between devices  18.1 us (11%)
    psum x1, blocking collectives, per_device(): totals = lax.psum(counts, ('sec', 'dev'))  78.6 us
    all_to_all x1, waiting for transfers between devices, per_device(): lax.all_to_all(expert_apply(lax.all_to_all(outgoing, ('sec', 'dev'), spli...  23.3 us
    all_to_all x1, starting transfers between devices, per_device(): lax.all_to_all(outgoing, ('sec', 'dev'), split_axis=0, concat_axis=0, til...  11.9 us
    dot_general x1, matrix products, expert_apply(): jnp.dot(flat_rows, w_gate_up[0], preferred_element_type=jnp.float32)  7.79 us
    dot_general x1, matrix products, expert_apply(): jnp.dot(activated, w_down[0], preferred_element_type=jnp.float32)  6.44 us
    all_to_all x1, starting transfers between devices, per_device(): lax.all_to_all(expert_apply(lax.all_to_all(outgoing, ('sec', 'dev'), spli...  6.24 us
    reshape x1, local copies, waits for them, and re-layouts, expert_apply(): flat_rows = received.reshape(-1, shape_in[-1])  4.91 us
    reshape x1, local copies, waits for them, and re-layouts, per_device(): picked = returned.reshape(experts * capacity, model_width)[slot_index]  4.91 us
  transfers between devices with their start and end apart: 2, of which 1 were waited for; matrix products, arithmetic and copies ran while one was open for 2% of the time, Pallas kernels for 0%

commit v1 on v0

v1 whole, which is shorter than its diff:
```python
import functools

import jax
import jax.numpy as jnp
from jax import lax
from jax.experimental import pallas as pl
from jax.experimental.pallas import tpu as pltpu
from jax.sharding import PartitionSpec as P

LANES = 128
BF16 = jnp.bfloat16
F32 = jnp.float32


def iota(shape, axis):
    return lax.broadcasted_iota(jnp.int32, shape, axis)


def packed_place(tile_row, blocks):
    within = tile_row & 7
    return (within >> 1) * (2 * blocks) + (tile_row >> 3) * 2 + (within & 1)


def to_rows_matrix(blocks):
    size = 8 * blocks
    return jnp.where(packed_place(iota((size, size), 0), blocks) == iota((size, size), 1), 1.0, 0.0).astype(BF16)


def to_chunks_matrix(blocks):
    size = 8 * blocks
    return jnp.where(packed_place(iota((size, size), 1), blocks) == iota((size, size), 0), 1.0, 0.0).astype(BF16)


def chunks_to_rows(chunk_ref, rows_ref, blocks):
    size = 8 * blocks
    matrix = to_rows_matrix(blocks)

    def step(group, carry):
        start = pl.multiple_of(group * (2 * size), 16)
        packed = chunk_ref[pl.ds(start, 2 * size), :].astype(F32)
        pair = jnp.concatenate([packed[:size], packed[size:]], axis=1).astype(BF16)
        spread = jnp.dot(matrix, pair, preferred_element_type=F32)
        row = pl.multiple_of(group * 16, 16)
        for block in range(blocks):
            piece = spread[8 * block : 8 * block + 8]
            rows_ref[pl.ds(row, 16), LANES * block : LANES * (block + 1)] = jnp.concatenate(
                [piece[:, :LANES], piece[:, LANES:]], axis=0
            ).astype(rows_ref.dtype)
        return carry

    lax.fori_loop(0, chunk_ref.shape[0] // (2 * size), step, 0)


def rows_to_chunks(rows_ref, chunk_ref, blocks):
    size = 8 * blocks
    matrix = to_chunks_matrix(blocks)

    def step(group, carry):
        row = pl.multiple_of(group * 16, 16)
        first = jnp.concatenate(
            [rows_ref[pl.ds(row, 8), LANES * b : LANES * (b + 1)] for b in range(blocks)], axis=0
        )
        second = jnp.concatenate(
            [rows_ref[pl.ds(row + 8, 8), LANES * b : LANES * (b + 1)] for b in range(blocks)], axis=0
        )
        pair = jnp.concatenate([first, second], axis=1).astype(BF16)
        packed = jnp.dot(matrix, pair, preferred_element_type=F32)
        start = pl.multiple_of(group * (2 * size), 16)
        chunk_ref[pl.ds(start, 2 * size), :] = jnp.concatenate(
            [packed[:, :LANES], packed[:, LANES:]], axis=0
        ).astype(BF16)
        return carry

    lax.fori_loop(0, chunk_ref.shape[0] // (2 * size), step, 0)


def choices(ids, values):
    lane = iota((ids.shape[0], LANES), 1)
    total = jnp.zeros((ids.shape[0], LANES), F32)
    for k in range(ids.shape[1]):
        total = total + jnp.where(ids[:, k : k + 1] == lane, values[k], 0.0)
    return total


def slot_of(chosen):
    rows = chosen.shape[0]
    before = jnp.where(iota((rows, rows), 1) < iota((rows, rows), 0), 1.0, 0.0).astype(BF16)
    return jnp.dot(before, chosen.astype(BF16), preferred_element_type=F32)


def interleave(first, second):
    experts = first.shape[1]
    expert, place = iota((experts, 2 * experts), 0), iota((experts, 2 * experts), 1)
    even = jnp.where(place == 2 * expert, 1.0, 0.0).astype(BF16)
    odd = jnp.where(place == 2 * expert + 1, 1.0, 0.0).astype(BF16)
    return jnp.dot(first.astype(BF16), even, preferred_element_type=F32) + jnp.dot(
        second.astype(BF16), odd, preferred_element_type=F32
    )


def dispatch_kernel(ids_ref, hidden_ref, chunk_ref, rows_ref):
    ids = ids_ref[...]
    width = hidden_ref.shape[1]
    chosen = choices(ids, [1.0] * ids.shape[1])
    slot = slot_of(chosen)
    placer = interleave(jnp.where(slot == 0.0, chosen, 0.0), jnp.where(slot == 1.0, chosen, 0.0))
    placer = jnp.transpose(placer).astype(BF16)
    rows_ref[:, :width] = jnp.dot(placer, hidden_ref[...], preferred_element_type=F32)
    counts = jnp.sum(chosen, axis=0, keepdims=True)
    rows_ref[:, width:] = jnp.broadcast_to(counts, (rows_ref.shape[0], LANES))
    rows_to_chunks(rows_ref, chunk_ref, rows_ref.shape[1] // LANES)


def expert_kernel(
    chunk_ref, up_hbm, down_hbm, out_ref, load_ref, up_ref, down_ref, rows_ref, act_ref, made_ref, up_sem, down_sem
):
    ups, downs = up_ref.shape[0], down_ref.shape[0]
    up_width, down_width = up_ref.shape[2], down_ref.shape[2]
    half = ups // 2
    width = up_ref.shape[1]

    def up_copy(c):
        return pltpu.make_async_copy(up_hbm.at[0, :, pl.ds(c * up_width, up_width)], up_ref.at[c], up_sem.at[c])

    def down_copy(c):
        return pltpu.make_async_copy(
            down_hbm.at[0, :, pl.ds(c * down_width, down_width)], down_ref.at[c], down_sem.at[c]
        )

    for c in range(half):
        up_copy(c).start()
        up_copy(c + half).start()
    for c in range(downs):
        down_copy(c).start()

    chunks_to_rows(chunk_ref, rows_ref, rows_ref.shape[1] // LANES)
    counts = jnp.sum(rows_ref[:, width:].astype(F32), axis=0, keepdims=True)
    load_ref[...] = counts * (0.5 / load_ref.shape[1])

    def up_step(c, carry):
        up_copy(c).wait()
        up_copy(c + half).wait()
        rows = rows_ref[:, :width]
        gate = jnp.dot(rows, up_ref[c], preferred_element_type=F32)
        up = jnp.dot(rows, up_ref[c + half], preferred_element_type=F32)
        place = pl.multiple_of(c * up_width, up_width)
        act_ref[:, pl.ds(place, up_width)] = (gate / (1.0 + jnp.exp(-gate)) * up).astype(BF16)
        return carry

    lax.fori_loop(0, half, up_step, 0)

    def down_step(c, carry):
        down_copy(c).wait()
        made = jnp.dot(act_ref[...], down_ref[c], preferred_element_type=F32)
        place = pl.multiple_of(c * down_width, down_width)
        made_ref[:, pl.ds(place, down_width)] = made
        return carry

    lax.fori_loop(0, downs, down_step, 0)
    rows_to_chunks(made_ref, out_ref, made_ref.shape[1] // LANES)


def combine_kernel(ids_ref, weights_ref, chunk_ref, out_ref, rows_ref):
    ids, weights = ids_ref[...], weights_ref[...]
    count = ids.shape[1]
    slot = slot_of(choices(ids, [1.0] * count))
    weight = choices(ids, [weights[:, k : k + 1] for k in range(count)])

    def parts(value):
        high = value.astype(BF16).astype(F32)
        return jnp.concatenate([high, value - high], axis=0)

    mixer = interleave(parts(jnp.where(slot == 0.0, weight, 0.0)), parts(jnp.where(slot == 1.0, weight, 0.0)))
    chunks_to_rows(chunk_ref, rows_ref, rows_ref.shape[1] // LANES)
    mixed = jnp.dot(mixer.astype(BF16), rows_ref[...], preferred_element_type=F32)
    rows = ids.shape[0]
    out_ref[...] = (mixed[:rows] + mixed[rows:]).astype(BF16)


def attend(query_latent, query_rope, latent_cache, rope_cache, cache_lengths):
    factor = (query_latent.shape[2] + query_rope.shape[1]) ** (-0.5)
    scores = jnp.einsum("rhc,rtc->rht", query_latent, latent_cache, preferred_element_type=F32)
    scores = scores + jnp.einsum("rph,rpt->rht", query_rope, rope_cache, preferred_element_type=F32)
    scores = scores * factor
    positions = jnp.arange(latent_cache.shape[1], dtype=jnp.int32)
    live_mask = positions[None, None, :] < cache_lengths[:, None, None]
    scores = jnp.where(live_mask, scores, -1e30)
    highest = jnp.max(scores, axis=-1, keepdims=True)
    powers = jnp.exp(scores - highest)
    attention_weights = (powers / jnp.sum(powers, axis=-1, keepdims=True)).astype(BF16)
    result = jnp.einsum("rht,rtc->rhc", attention_weights, latent_cache, preferred_element_type=F32)
    return result.astype(BF16)


def vmem(count):
    return [pl.BlockSpec(memory_space=pltpu.VMEM)] * count


def exchange(chunks, experts):
    width = chunks.shape[1]
    shaped = chunks.reshape(experts, -1, 2, width)
    moved = lax.all_to_all(shaped, ("sec", "dev"), split_axis=0, concat_axis=0, tiled=True)
    return moved.reshape(chunks.shape)


def per_device(
    hidden,
    expert_ids,
    route_weights,
    w_gate_up,
    w_down,
    query_latent,
    query_rope,
    latent_cache,
    rope_cache,
    cache_lengths,
):
    model_width = hidden.shape[1]
    experts = lax.axis_size("sec") * lax.axis_size("dev")
    slots = 2 * experts
    units = w_down.shape[1]
    blocks = model_width // LANES
    sent = blocks + 1

    outgoing = pl.pallas_call(
        dispatch_kernel,
        out_shape=jax.ShapeDtypeStruct((slots * sent, LANES), BF16),
        in_specs=vmem(2),
        out_specs=pl.BlockSpec(memory_space=pltpu.VMEM),
        scratch_shapes=[pltpu.VMEM((slots, sent * LANES), F32)],
        compiler_params=pltpu.CompilerParams(vmem_limit_bytes=16 << 20),
        name="dispatch",
    )(expert_ids, hidden)
    received = exchange(outgoing, experts)

    up_width, down_width = 256, 512
    ups, downs = 2 * units // up_width, model_width // down_width
    returned, load = pl.pallas_call(
        expert_kernel,
        out_shape=(
            jax.ShapeDtypeStruct((slots * blocks, LANES), BF16),
            jax.ShapeDtypeStruct((1, experts), F32),
        ),
        in_specs=vmem(1) + [pl.BlockSpec(memory_space=pl.ANY)] * 2,
        out_specs=tuple(vmem(2)),
        scratch_shapes=[
            pltpu.VMEM((ups, model_width, up_width), BF16),
            pltpu.VMEM((downs, units, down_width), BF16),
            pltpu.VMEM((slots, sent * LANES), BF16),
            pltpu.VMEM((slots, units), BF16),
            pltpu.VMEM((slots, model_width), F32),
            pltpu.SemaphoreType.DMA((ups,)),
            pltpu.SemaphoreType.DMA((downs,)),
        ],
        compiler_params=pltpu.CompilerParams(vmem_limit_bytes=48 << 20),
        name="experts",
    )(received, w_gate_up, w_down)
    collected = exchange(returned, experts)

    moe_out = pl.pallas_call(
        combine_kernel,
        out_shape=jax.ShapeDtypeStruct(hidden.shape, BF16),
        in_specs=vmem(3),
        out_specs=pl.BlockSpec(memory_space=pltpu.VMEM),
        scratch_shapes=[pltpu.VMEM((slots, model_width), BF16)],
        compiler_params=pltpu.CompilerParams(vmem_limit_bytes=16 << 20),
        name="combine",
    )(expert_ids, route_weights, collected)
    attention_out = attend(query_latent, query_rope, latent_cache, rope_cache, cache_lengths)
    return (moe_out, load[0], attention_out)


def solution(mesh):
    split = ("sec", "dev")
    return jax.shard_map(
        per_device,
        mesh=mesh,
        in_specs=(
            P(split, None),
            P(split, None),
            P(split, None),
            P(split, None, None),
            P(split, None, None),
            P(split, None, None),
            P(split, None, None),
            P(split, None, None),
            P(split, None, None),
            P(split),
        ),
        out_specs=(P(split, None), P(), P(split, None, None)),
        check_vma=False,
    )
```

time: 168 us -> 101 us (0.60)
  blocking collectives: 78.6 us -> 39.6 us
  Pallas kernels: 0 us -> 24.8 us
  local copies, waits for them, and re-layouts: 25 us -> 3.13 us
  matrix products: 20.4 us -> 3.02 us
  starting transfers between devices: 18.1 us -> 5.54 us
    psum x1 -> x0, blocking collectives: 78.6 us -> none  [per_device(): totals = lax.psum(counts, ('sec', 'dev'))]
    all_to_all x0 -> x1, blocking collectives: none -> 39.6 us  [exchange(): lax.all_to_all(shaped, ('sec', 'dev'), split_axis=0, concat_axis=0, tiled...]
    pallas_call x0 -> x3, Pallas kernels: none -> 24.8 us  [the longest x1 14.8 us: per_device(): pl.pallas_call(expert_kernel, out_shape=(jax.ShapeDtypeStruct((slots * bl...]
    reshape x4 -> x0, local copies, waits for them, and re-layouts: 19.3 us -> none  [the longest x1 4.91 us: expert_apply(): flat_rows = received.reshape(-1, shape_in[-1])]
    dot_general x4 -> x0, matrix products: 17.4 us -> none  [the longest x1 7.79 us: expert_apply(): jnp.dot(flat_rows, w_gate_up[0], preferred_element_type=jnp.float32)]
    all_to_all x2 -> x1, starting transfers between devices: 18.1 us -> 5.54 us  [exchange(): lax.all_to_all(shaped, ('sec', 'dev'), split_axis=0, concat_axis=0, tiled...]
    gather x1 -> x0, local copies, waits for them, and re-layouts: 3.76 us -> none  [per_device(): picked = returned.reshape(experts * capacity, model_width)[slot_index]]
    unnamed x14 -> x18, local copies, waits for them, and re-layouts: 1.02 us -> 3.13 us
  transfers between devices with their start and end apart: 2 -> 1, of which waited for: 1 -> 1; matrix products, arithmetic and copies ran while one was open for 2% -> 3% of each run, Pallas kernels for 0% -> 0%
where the time goes in v1:
time: 101 us
  blocking collectives  39.6 us (39%)
  Pallas kernels  24.8 us (25%)
  waiting for transfers between devices  23.9 us (24%)
  starting transfers between devices  5.54 us (5%)
  local copies, waits for them, and re-layouts  3.13 us (3%)
  matrix products  3.02 us (3%)
    all_to_all x1, blocking collectives, exchange(): lax.all_to_all(shaped, ('sec', 'dev'), split_axis=0, concat_axis=0, tiled...  39.6 us
    all_to_all x1, waiting for transfers between devices, exchange(): lax.all_to_all(shaped, ('sec', 'dev'), split_axis=0, concat_axis=0, tiled...  23.9 us
    pallas_call x1, Pallas kernels, per_device(): pl.pallas_call(expert_kernel, out_shape=(jax.ShapeDtypeStruct((slots * bl...  14.8 us
    pallas_call x1, Pallas kernels, per_device(): pl.pallas_call(combine_kernel, out_shape=jax.ShapeDtypeStruct(hidden.shap...  5.86 us
    all_to_all x1, starting transfers between devices, exchange(): lax.all_to_all(shaped, ('sec', 'dev'), split_axis=0, concat_axis=0, tiled...  5.54 us
    pallas_call x1, Pallas kernels, per_device(): pl.pallas_call(dispatch_kernel, out_shape=jax.ShapeDtypeStruct((slots * s...  4.1 us
    unnamed x18, local copies, waits for them, and re-layouts  3.13 us
  transfers between devices with their start and end apart: 1, of which 1 were waited for; matrix products, arithmetic and copies ran while one was open for 3% of the time, Pallas kernels for 0%

profile of v1, /device:TPU:1, one launch (start us, length us, event | category | flops | bytes accessed | tf_op | source)
XLA Modules:
  0.0 101.2 jit_solution(5095699634345871899)
XLA Ops:
  0.6 0.0 copy-start
  0.6 0.9 copy.14.ids_ref
  1.6 0.0 copy-start.2
  1.6 0.9 copy-done.2
  2.5 4.1 %dispatch.1 = bf16[7424,128]{1,0:T(8,128)(2,1)S(1)} custom-call(s32[16,8]{1,0:T(8,128)S(1)} %copy.14.ids_ref, bf16[16,3584]{1,0:T(8,128)(2,1)S(1)} %copy-done.2), custom_call_target="tpu_custom_call" | custom-call | tf_op jit(solution)/shard_map/dispatch/pallas_call | solution.py:225
  6.6 39.6 %all_to_all.10 = bf16[128,29,2,128]{3,2,1,0:T(2,128)(2,1)S(1)} all-to-all(bf16[128,29,2,128]{3,2,1,0:T(2,128)(2,1)S(1)} %bitcast.12), channel_id=1, replica_groups=mesh['sec'=4,'dev'=32] {'sec','dev'}, dimensions={0} | all-to-all | bytes 3801088 | tf_op jit(solution)/shard_map/all_to_all | solution.py:202
  46.2 14.8 %experts.1 = (bf16[7168,128]{1,0:T(8,128)(2,1)S(1)}, f32[1,128]{1,0:T(1,128)}) custom-call(bf16[7424,128]{1,0:T(8,128)(2,1)S(1)} %bitcast.13, bf16[1,3584,2048]{2,1,0:T(8,128)(2,1)} %up_hbm.1, bf16[1,1024,3584]{2,1,0:T(8,128)(2,1)} %down_hbm.1), custom_call_target="tpu_custom_call" | custom-call | tf_op jit(solution)/shard_map/experts/pallas_call | solution.py:238
  61.0 0.0 copy-start.1
  61.1 1.2 %copy-done.1 = bf16[7168,128]{1,0:T(8,128)(2,1)} copy-done((bf16[7168,128]{1,0:T(8,128)(2,1)}, bf16[7168,128]{1,0:T(8,128)(2,1)S(1)}, u32[]{:S(2)}) %copy-start.1) | copy-done | bytes 1835032
  62.3 0.0 copy-start.6
  62.3 0.0 copy-start.7
  62.3 0.0 copy-start.3
  62.3 5.5 %all-to-all-start.1 = ((bf16[128,28,2,128]{3,2,1,0:T(2,128)(2,1)}), bf16[128,28,2,128]{3,2,1,0:T(2,128)(2,1)}, u32[]{:S(2)}, u32[]{:S(2)}) async-start(bf16[128,28,2,128]{3,2,1,0:T(2,128)(2,1)} %bitcast.14), calls=%async_computation.1 | async-start | bytes 3670016 | tf_op jit(solution)/shard_map/all_to_all | solution.py:202
  67.8 0.0 copy-done.6
  67.8 0.0 copy-start.4
  67.8 0.0 copy-start.5
  67.9 0.1 copy.15.weights_ref
  67.9 0.0 copy-done.7
  67.9 0.1 iota_compare_fusion
  68.0 0.0 copy-done
  68.0 0.0 copy-done.3
  68.0 0.8 fusion.8
  68.8 0.0 copy-done.4
  68.8 0.0 copy-done.5
  68.9 0.4 fusion.4
  69.2 0.3 fusion.7
  69.5 1.9 %convolution_convert_fusion = bf16[4,128,512]{2,1,0:T(8,128)(2,1)} fusion(bf16[4,512,512]{2,1,0:T(8,128)(2,1)S(1)} %copy-done, f32[4,128]{1,0:T(4,128)S(1)} %fusion.7, f32[4,128,512]{2,1,0:T(8,128)S(1)} %fusion.4), kind=kOutput, calls=%fused_computation.6 | convolution fusion | flops 269485056 | bytes 3672064 | tf_op jit(solution)/shard_map/rht,rtc->rhc/dot_general | solution.py:191
  71.4 23.9 %all-to-all-done.1 = bf16[128,28,2,128]{3,2,1,0:T(2,128)(2,1)} async-done(((bf16[128,28,2,128]{3,2,1,0:T(2,128)(2,1)}), bf16[128,28,2,128]{3,2,1,0:T(2,128)(2,1)}, u32[]{:S(2)}, u32[]{:S(2)}) %all-to-all-start.1) | async-done | bytes 1835040 | tf_op jit(solution)/shard_map/all_to_all | solution.py:202
  95.3 5.9 %combine.1 = bf16[16,3584]{1,0:T(8,128)(2,1)} custom-call(s32[16,8]{1,0:T(8,128)S(1)} %copy.14.ids_ref, f32[16,8]{1,0:T(8,128)S(1)} %copy.15.weights_ref, bf16[7168,128]{1,0:T(8,128)(2,1)} %bitcast.3.chunk_ref), custom_call_target="tpu_custom_call" | custom-call | tf_op jit(solution)/shard_map/combine/pallas_call | solution.py:260
Async XLA Ops:
  0.6 67.4 %copy-start = (bf16[4,512,512]{2,1,0:T(8,128)(2,1)S(1)}, bf16[4,512,512]{2,1,0:T(8,128)(2,1)}, u32[]{:S(2)}) copy-start(bf16[4,512,512]{2,1,0:T(8,128)(2,1)} %param.17) | copy-start | bytes 6291460
  1.6 0.9 copy-start.2
  61.0 1.2 %copy-start.1 = (bf16[7168,128]{1,0:T(8,128)(2,1)}, bf16[7168,128]{1,0:T(8,128)(2,1)S(1)}, u32[]{:S(2)}) copy-start(bf16[7168,128]{1,0:T(8,128)(2,1)S(1)} %get-tuple-element.5) | copy-start | bytes 5505028
  62.3 5.6 %copy-start.6 = (f32[16,8]{0,1:T(8,128)S(1)}, f32[16,8]{0,1:T(8,128)}, u32[]{:S(2)}) copy-start(f32[16,8]{0,1:T(8,128)} %param.12) | copy-start | bytes 1540
  62.3 5.7 %copy-start.7 = (s32[4]{0:T(128)S(1)}, s32[4]{0:T(128)}, u32[]{:S(2)}) copy-start(s32[4]{0:T(128)} %param.19) | copy-start | bytes 52
  62.3 5.7 %copy-start.3 = (bf16[4,128,512]{2,1,0:T(8,128)(2,1)S(1)}, bf16[4,128,512]{2,1,0:T(8,128)(2,1)}, u32[]{:S(2)}) copy-start(bf16[4,128,512]{2,1,0:T(8,128)(2,1)} %param.15) | copy-start | bytes 1572868
  62.3 33.0 %all-to-all-start.1 = ((bf16[128,28,2,128]{3,2,1,0:T(2,128)(2,1)}), bf16[128,28,2,128]{3,2,1,0:T(2,128)(2,1)}, u32[]{:S(2)}, u32[]{:S(2)}) async-start(bf16[128,28,2,128]{3,2,1,0:T(2,128)(2,1)} %bitcast.14), calls=%async_computation.1 | async-start | bytes 3670016 | tf_op jit(solution)/shard_map/all_to_all | solution.py:202
  67.8 1.0 copy-start.4
  67.8 1.0 copy-start.5

commit v2 on v1

v2 whole, which is shorter than its diff:
```python
import jax
import jax.numpy as jnp
from jax import lax
from jax.experimental import pallas as pl
from jax.experimental.pallas import tpu as pltpu
from jax.sharding import Mesh, PartitionSpec as P

LANES = 128
BF16 = jnp.bfloat16
F32 = jnp.float32
IN_FLIGHT = 6
AXES = ("core", "y", "x", "z")


def iota(shape, axis):
    return lax.broadcasted_iota(jnp.int32, shape, axis)


def packed_place(tile_row, blocks):
    within = tile_row & 7
    return (within >> 1) * (2 * blocks) + (tile_row >> 3) * 2 + (within & 1)


def to_rows_matrix(blocks):
    size = 8 * blocks
    return jnp.where(packed_place(iota((size, size), 0), blocks) == iota((size, size), 1), 1.0, 0.0).astype(BF16)


def to_chunks_matrix(blocks):
    size = 8 * blocks
    return jnp.where(packed_place(iota((size, size), 1), blocks) == iota((size, size), 0), 1.0, 0.0).astype(BF16)


def chunks_to_rows(chunk_ref, rows_ref, blocks, before=None):
    size = 8 * blocks
    matrix = to_rows_matrix(blocks)
    for group in range(chunk_ref.shape[0] // (2 * size)):
        if before is not None:
            before(group)
        start, row = group * (2 * size), group * 16
        packed = chunk_ref[start : start + 2 * size, :].astype(F32)
        pair = jnp.concatenate([packed[:size], packed[size:]], axis=1).astype(BF16)
        spread = jnp.dot(matrix, pair, preferred_element_type=F32)
        for block in range(blocks):
            piece = spread[8 * block : 8 * block + 8]
            rows_ref[row : row + 16, LANES * block : LANES * (block + 1)] = jnp.concatenate(
                [piece[:, :LANES], piece[:, LANES:]], axis=0
            ).astype(rows_ref.dtype)


def rows_to_chunks(rows_ref, chunk_ref, blocks, after=None):
    size = 8 * blocks
    matrix = to_chunks_matrix(blocks)
    for group in range(chunk_ref.shape[0] // (2 * size)):
        start, row = group * (2 * size), group * 16
        halves = [
            jnp.concatenate(
                [rows_ref[first : first + 8, LANES * b : LANES * (b + 1)] for b in range(blocks)], axis=0
            )
            for first in (row, row + 8)
        ]
        packed = jnp.dot(matrix, jnp.concatenate(halves, axis=1).astype(BF16), preferred_element_type=F32)
        chunk_ref[start : start + 2 * size, :] = jnp.concatenate(
            [packed[:, :LANES], packed[:, LANES:]], axis=0
        ).astype(BF16)
        if after is not None:
            after(group)


def choices(ids, values):
    lane = iota((ids.shape[0], LANES), 1).astype(ids.dtype)
    total = jnp.zeros((ids.shape[0], LANES), F32)
    for k in range(ids.shape[1]):
        total = total + jnp.where(ids[:, k : k + 1] == lane, values[k], 0.0)
    return total


def rank_of(ids):
    ids = ids.astype(jnp.int32)
    core, x, z, y = ids & 1, (ids >> 1) & 3, (ids >> 3) & 3, ids >> 5
    return ((core * 4 + y) * 4 + x) * 4 + z


def slot_of(chosen):
    rows = chosen.shape[0]
    before = jnp.where(iota((rows, rows), 1) < iota((rows, rows), 0), 1.0, 0.0).astype(BF16)
    return jnp.dot(before, chosen.astype(BF16), preferred_element_type=F32)


def interleave(first, second):
    experts = first.shape[1]
    expert, place = iota((experts, 2 * experts), 0), iota((experts, 2 * experts), 1)
    even = jnp.where(place == 2 * expert, 1.0, 0.0).astype(BF16)
    odd = jnp.where(place == 2 * expert + 1, 1.0, 0.0).astype(BF16)
    return jnp.dot(first.astype(BF16), even, preferred_element_type=F32) + jnp.dot(
        second.astype(BF16), odd, preferred_element_type=F32
    )


def dispatch_kernel(ids_hbm, hidden_hbm, chunk_ref, ids_ref, hidden_ref, rows_ref, sem):
    ids_copy = pltpu.make_async_copy(ids_hbm, ids_ref, sem.at[0])
    hidden_copy = pltpu.make_async_copy(hidden_hbm, hidden_ref, sem.at[1])
    ids_copy.start()
    hidden_copy.start()
    ids_copy.wait()
    count = ids_ref.shape[0]
    ids = jnp.transpose(ids_ref[...].astype(F32))
    width = hidden_ref.shape[1]
    counts = jnp.sum(choices(ids, [1.0] * count), axis=0, keepdims=True)
    chosen = choices(rank_of(ids), [1.0] * count)
    slot = slot_of(chosen)
    placer = interleave(jnp.where(slot == 0.0, chosen, 0.0), jnp.where(slot == 1.0, chosen, 0.0))
    placer = jnp.transpose(placer).astype(BF16)
    rows_ref[:, width:] = jnp.broadcast_to(counts, (rows_ref.shape[0], LANES))
    hidden_copy.wait()
    rows_ref[:, :width] = jnp.dot(placer, hidden_ref[...], preferred_element_type=F32)
    rows_to_chunks(rows_ref, chunk_ref, rows_ref.shape[1] // LANES)


def expert_kernel(
    chunk_ref,
    up_hbm,
    down_hbm,
    out_hbm,
    load_ref,
    up_ref,
    down_ref,
    rows_ref,
    act_ref,
    made_ref,
    out_ref,
    weight_sem,
    out_sem,
):
    ups, downs = up_ref.shape[0], down_ref.shape[0]
    up_width, down_width = up_ref.shape[2], down_ref.shape[2]
    half = ups // 2
    width = up_ref.shape[1]

    copies = []
    for c in range(half):
        for part in (c, c + half):
            copies.append((up_hbm.at[0, :, pl.ds(part * up_width, up_width)], up_ref.at[part]))
    for c in range(downs):
        copies.append((down_hbm.at[0, :, pl.ds(c * down_width, down_width)], down_ref.at[c]))
    copies = [pltpu.make_async_copy(*pair, weight_sem.at[n]) for n, pair in enumerate(copies)]
    for copy in copies[:IN_FLIGHT]:
        copy.start()

    def arrive(n):
        copies[n].wait()
        if n + IN_FLIGHT < len(copies):
            copies[n + IN_FLIGHT].start()

    chunks_to_rows(chunk_ref, rows_ref, rows_ref.shape[1] // LANES)
    counts = jnp.sum(rows_ref[:, width:].astype(F32), axis=0, keepdims=True)
    load_ref[...] = counts * (0.5 / load_ref.shape[1])

    for c in range(half):
        arrive(2 * c)
        arrive(2 * c + 1)
        rows = rows_ref[:, :width]
        gate = jnp.dot(rows, up_ref[c], preferred_element_type=F32)
        up = jnp.dot(rows, up_ref[c + half], preferred_element_type=F32)
        act_ref[:, c * up_width : (c + 1) * up_width] = (gate / (1.0 + jnp.exp(-gate)) * up).astype(BF16)

    for c in range(downs):
        arrive(ups + c)
        made_ref[:, c * down_width : (c + 1) * down_width] = jnp.dot(
            act_ref[...], down_ref[c], preferred_element_type=F32
        )

    blocks = made_ref.shape[1] // LANES
    span = 4 * 16 * blocks
    leave = [
        pltpu.make_async_copy(
            out_ref.at[pl.ds(n * span, span), :], out_hbm.at[pl.ds(n * span, span), :], out_sem.at[n]
        )
        for n in range(out_ref.shape[0] // span)
    ]

    def after(group):
        if group % 4 == 3:
            leave[group // 4].start()

    rows_to_chunks(made_ref, out_ref, blocks, after)
    for copy in leave:
        copy.wait()


def combine_kernel(ids_ref, weights_ref, chunk_hbm, out_ref, chunk_ref, rows_ref, sem):
    blocks = rows_ref.shape[1] // LANES
    span = 4 * 16 * blocks
    enter = [
        pltpu.make_async_copy(
            chunk_hbm.at[pl.ds(n * span, span), :], chunk_ref.at[pl.ds(n * span, span), :], sem.at[n]
        )
        for n in range(chunk_ref.shape[0] // span)
    ]
    for copy in enter:
        copy.start()
    ids, weights = jnp.transpose(ids_ref[...].astype(F32)), jnp.transpose(weights_ref[...])
    count = ids.shape[1]
    ids = rank_of(ids)
    slot = slot_of(choices(ids, [1.0] * count))
    weight = choices(ids, [weights[:, k : k + 1] for k in range(count)])

    def parts(value):
        high = value.astype(BF16).astype(F32)
        return jnp.concatenate([high, value - high], axis=0)

    mixer = interleave(parts(jnp.where(slot == 0.0, weight, 0.0)), parts(jnp.where(slot == 1.0, weight, 0.0)))

    def before(group):
        if group % 4 == 0:
            enter[group // 4].wait()

    chunks_to_rows(chunk_ref, rows_ref, blocks, before)
    mixed = jnp.dot(mixer.astype(BF16), rows_ref[...], preferred_element_type=F32)
    rows = ids.shape[0]
    out_ref[...] = (mixed[:rows] + mixed[rows:]).astype(BF16)


def attend(query_latent, query_rope, latent_cache, rope_cache, cache_lengths):
    factor = (query_latent.shape[2] + query_rope.shape[1]) ** (-0.5)
    scores = jnp.einsum("rhc,rtc->rht", query_latent, latent_cache, preferred_element_type=F32)
    scores = scores + jnp.einsum("rph,rpt->rht", query_rope, rope_cache, preferred_element_type=F32)
    scores = scores * factor
    positions = jnp.arange(latent_cache.shape[1], dtype=jnp.int32)
    live_mask = positions[None, None, :] < cache_lengths[:, None, None]
    scores = jnp.where(live_mask, scores, -1e30)
    highest = jnp.max(scores, axis=-1, keepdims=True)
    powers = jnp.exp(scores - highest)
    attention_weights = (powers / jnp.sum(powers, axis=-1, keepdims=True)).astype(BF16)
    result = jnp.einsum("rht,rtc->rhc", attention_weights, latent_cache, preferred_element_type=F32)
    return result.astype(BF16)


def vmem(count):
    return [pl.BlockSpec(memory_space=pltpu.VMEM)] * count


def hbm(count):
    return [pl.BlockSpec(memory_space=pltpu.HBM)] * count


def exchange(chunks, experts):
    width = chunks.shape[1]
    shaped = chunks.reshape(experts, -1, 2, width)
    moved = lax.all_to_all(shaped, AXES, split_axis=0, concat_axis=0, tiled=True)
    return moved.reshape(chunks.shape)


def per_device(
    hidden,
    expert_ids,
    route_weights,
    w_gate_up,
    w_down,
    query_latent,
    query_rope,
    latent_cache,
    rope_cache,
    cache_lengths,
):
    model_width = hidden.shape[1]
    experts = lax.axis_size(AXES)
    slots = 2 * experts
    units = w_down.shape[1]
    blocks = model_width // LANES
    sent = blocks + 1

    outgoing = pl.pallas_call(
        dispatch_kernel,
        out_shape=jax.ShapeDtypeStruct((slots * sent, LANES), BF16),
        in_specs=hbm(2),
        out_specs=pl.BlockSpec(memory_space=pltpu.VMEM),
        scratch_shapes=[
            pltpu.VMEM(expert_ids.shape[::-1], jnp.int32),
            pltpu.VMEM(hidden.shape, BF16),
            pltpu.VMEM((slots, sent * LANES), F32),
            pltpu.SemaphoreType.DMA((2,)),
        ],
        compiler_params=pltpu.CompilerParams(vmem_limit_bytes=65_110_016),
        name="dispatch",
    )(expert_ids.T, hidden)
    received = exchange(outgoing, experts)

    up_width, down_width = 256, 512
    ups, downs = 2 * units // up_width, model_width // down_width
    returned, load = pl.pallas_call(
        expert_kernel,
        out_shape=(
            jax.ShapeDtypeStruct((slots * blocks, LANES), BF16),
            jax.ShapeDtypeStruct((1, experts), F32),
        ),
        in_specs=vmem(1) + hbm(2),
        out_specs=tuple(hbm(1) + vmem(1)),
        scratch_shapes=[
            pltpu.VMEM((ups, model_width, up_width), BF16),
            pltpu.VMEM((downs, units, down_width), BF16),
            pltpu.VMEM((slots, sent * LANES), BF16),
            pltpu.VMEM((slots, units), BF16),
            pltpu.VMEM((slots, model_width), F32),
            pltpu.VMEM((slots * blocks, LANES), BF16),
            pltpu.SemaphoreType.DMA((ups + downs,)),
            pltpu.SemaphoreType.DMA((4,)),
        ],
        compiler_params=pltpu.CompilerParams(vmem_limit_bytes=60 * 1024 * 1024),
        name="experts",
    )(received, w_gate_up, w_down)
    collected = exchange(returned, experts)

    moe_out = pl.pallas_call(
        combine_kernel,
        out_shape=jax.ShapeDtypeStruct(hidden.shape, BF16),
        in_specs=vmem(2) + hbm(1),
        out_specs=pl.BlockSpec(memory_space=pltpu.VMEM),
        scratch_shapes=[
            pltpu.VMEM((slots * blocks, LANES), BF16),
            pltpu.VMEM((slots, model_width), BF16),
            pltpu.SemaphoreType.DMA((4,)),
        ],
        compiler_params=pltpu.CompilerParams(vmem_limit_bytes=16 << 20),
        name="combine",
    )(expert_ids.T, route_weights.T, collected)
    attention_out = attend(query_latent, query_rope, latent_cache, rope_cache, cache_lengths)
    return (moe_out, load[0], attention_out)


def solution(mesh):
    split = ("y", "z", "x", "core")
    mesh = Mesh(mesh.devices.reshape(4, 4, 4, 2), split)
    return jax.shard_map(
        per_device,
        mesh=mesh,
        in_specs=(
            P(split, None),
            P(split, None),
            P(split, None),
            P(split, None, None),
            P(split, None, None),
            P(split, None, None),
            P(split, None, None),
            P(split, None, None),
            P(split, None, None),
            P(split),
        ),
        out_specs=(P(split, None), P(), P(split, None, None)),
        check_vma=False,
    )
```

time: 101 us -> 91.6 us (0.907)
  Pallas kernels: 24.8 us -> 20.4 us
  waiting for transfers between devices: 23.9 us -> 20.2 us
  local copies, waits for them, and re-layouts: 3.13 us -> 0.09 us
  blocking collectives: 39.6 us -> 38 us
  matrix products: 3.02 us -> 4.61 us
  starting transfers between devices: 5.54 us -> 6.88 us
    all_to_all x1, waiting for transfers between devices: 23.9 us -> 20.2 us  [exchange(): lax.all_to_all(shaped, AXES, split_axis=0, concat_axis=0, tiled=True)]
    unnamed x18 -> x14, local copies, waits for them, and re-layouts: 3.13 us -> 0.09 us
    pallas_call x1, Pallas kernels: 5.86 us -> 3.21 us  [per_device(): pl.pallas_call(combine_kernel, out_shape=jax.ShapeDtypeStruct(hidden.shap...]
    all_to_all x1, blocking collectives: 39.6 us -> 38 us  [exchange(): lax.all_to_all(shaped, AXES, split_axis=0, concat_axis=0, tiled=True)]
    dot_general x1, matrix products: 1.86 us -> 3.45 us  [attend(): jnp.einsum('rht,rtc->rhc', attention_weights, latent_cache, preferred_ele...]
    pallas_call x1, Pallas kernels: 14.8 us -> 13.4 us  [per_device(): pl.pallas_call(expert_kernel, out_shape=(jax.ShapeDtypeStruct((slots * bl...]
    all_to_all x1, starting transfers between devices: 5.54 us -> 6.88 us  [exchange(): lax.all_to_all(shaped, AXES, split_axis=0, concat_axis=0, tiled=True)]
  transfers between devices with their start and end apart: 1 -> 1, of which waited for: 1 -> 1; matrix products, arithmetic and copies ran while one was open for 3% -> 5% of each run, Pallas kernels for 0% -> 0%
where the time goes in v2:
time: 91.6 us; the launch traced here: 91.3 us
  blocking collectives  38 us (41%)
  Pallas kernels  20.4 us (22%)
  waiting for transfers between devices  20.2 us (22%)
  starting transfers between devices  6.88 us (8%)
  matrix products  4.61 us (5%)
    all_to_all x1, blocking collectives, exchange(): lax.all_to_all(shaped, AXES, split_axis=0, concat_axis=0, tiled=True)  38 us
    all_to_all x1, waiting for transfers between devices, exchange(): lax.all_to_all(shaped, AXES, split_axis=0, concat_axis=0, tiled=True)  20.2 us
    pallas_call x1, Pallas kernels, per_device(): pl.pallas_call(expert_kernel, out_shape=(jax.ShapeDtypeStruct((slots * bl...  13.4 us
    all_to_all x1, starting transfers between devices, exchange(): lax.all_to_all(shaped, AXES, split_axis=0, concat_axis=0, tiled=True)  6.88 us
    pallas_call x1, Pallas kernels, per_device(): pl.pallas_call(dispatch_kernel, out_shape=jax.ShapeDtypeStruct((slots * s...  3.73 us
    dot_general x1, matrix products, attend(): jnp.einsum('rht,rtc->rhc', attention_weights, latent_cache, preferred_ele...  3.45 us
    pallas_call x1, Pallas kernels, per_device(): pl.pallas_call(combine_kernel, out_shape=jax.ShapeDtypeStruct(hidden.shap...  3.21 us
  transfers between devices with their start and end apart: 1, of which 1 were waited for; matrix products, arithmetic and copies ran while one was open for 5% of the time, Pallas kernels for 0%

profile of v2, /device:TPU:1, one launch (start us, length us, event | category | flops | bytes accessed | tf_op | source)
XLA Modules:
  0.0 91.3 jit_solution(18103506108906415950)
XLA Ops:
  0.6 0.0 copy-start
  0.6 3.7 %dispatch.1 = bf16[7424,128]{1,0:T(8,128)(2,1)} custom-call(s32[8,16]{1,0:T(8,128)} %bitcast.14, bf16[16,3584]{1,0:T(8,128)(2,1)} %hidden_hbm.1), custom_call_target="tpu_custom_call" | custom-call | tf_op jit(solution)/shard_map/dispatch/pallas_call | solution.py:273
  4.4 38.0 %all_to_all.10 = bf16[128,29,2,128]{3,2,1,0:T(2,128)(2,1)} all-to-all(bf16[128,29,2,128]{3,2,1,0:T(2,128)(2,1)} %bitcast.17), channel_id=1, replica_groups=mesh['y'=4,'z'=4,'x'=4,'core'=2] {'core','y','x','z'}, dimensions={0} | all-to-all | bytes 3801088 | tf_op jit(solution)/shard_map/all_to_all | solution.py:250
  42.4 13.4 %experts.1 = (bf16[7168,128]{1,0:T(8,128)(2,1)}, f32[1,128]{1,0:T(1,128)}) custom-call(bf16[7424,128]{1,0:T(8,128)(2,1)} %bitcast.18, bf16[1,3584,2048]{2,1,0:T(8,128)(2,1)} %up_hbm.1, bf16[1,1024,3584]{2,1,0:T(8,128)(2,1)} %down_hbm.1), custom_call_target="tpu_custom_call" | custom-call | tf_op jit(solution)/shard_map/experts/pallas_call | solution.py:291
  55.8 0.0 copy-start.6
  55.8 0.0 copy-start.3
  55.8 6.9 %all-to-all-start.1 = ((bf16[128,28,2,128]{3,2,1,0:T(2,128)(2,1)}), bf16[128,28,2,128]{3,2,1,0:T(2,128)(2,1)}, u32[]{:S(2)}, u32[]{:S(2)}) async-start(bf16[128,28,2,128]{3,2,1,0:T(2,128)(2,1)} %bitcast.19), calls=%async_computation.1 | async-start | bytes 3670016 | tf_op jit(solution)/shard_map/all_to_all | solution.py:250
  62.7 0.0 copy-done.6
  62.7 0.0 copy-start.4
  62.7 0.0 copy-start.5
  62.7 0.1 iota_compare_fusion
  62.8 0.0 copy-done
  62.8 0.0 copy-done.3
  62.8 0.8 fusion.8
  63.6 0.0 copy-done.4
  63.7 0.0 copy-done.5
  63.7 0.4 fusion.4
  64.0 0.3 fusion.7
  64.4 0.0 copy-start.1
  64.4 0.0 copy-start.2
  64.4 3.5 %convolution_convert_fusion = bf16[4,128,512]{2,1,0:T(8,128)(2,1)} fusion(bf16[4,512,512]{2,1,0:T(8,128)(2,1)} %param.17, f32[4,128]{1,0:T(4,128)S(1)} %fusion.7, f32[4,128,512]{2,1,0:T(8,128)S(1)} %fusion.4), kind=kOutput, calls=%fused_computation.6 | convolution fusion | flops 269485056 | bytes 3672064 | tf_op jit(solution)/shard_map/rht,rtc->rhc/dot_general | solution.py:235
  67.8 20.2 %all-to-all-done.1 = bf16[128,28,2,128]{3,2,1,0:T(2,128)(2,1)} async-done(((bf16[128,28,2,128]{3,2,1,0:T(2,128)(2,1)}), bf16[128,28,2,128]{3,2,1,0:T(2,128)(2,1)}, u32[]{:S(2)}, u32[]{:S(2)}) %all-to-all-start.1) | async-done | bytes 1835040 | tf_op jit(solution)/shard_map/all_to_all | solution.py:250
  88.0 0.0 copy-done.1
  88.0 0.0 copy-done.2
  88.0 3.2 %combine.1 = bf16[16,3584]{1,0:T(8,128)(2,1)} custom-call(s32[8,16]{1,0:T(8,128)S(1)} %bitcast.15, f32[8,16]{1,0:T(8,128)S(1)} %bitcast.16, bf16[7168,128]{1,0:T(8,128)(2,1)} %bitcast.5.chunk_hbm), custom_call_target="tpu_custom_call" | custom-call | tf_op jit(solution)/shard_map/combine/pallas_call | solution.py:314
Async XLA Ops:
  0.6 62.2 %copy-start = (bf16[4,128,512]{2,1,0:T(8,128)(2,1)S(1)}, bf16[4,128,512]{2,1,0:T(8,128)(2,1)}, u32[]{:S(2)}) copy-start(bf16[4,128,512]{2,1,0:T(8,128)(2,1)} %param.15) | copy-start | bytes 1572868
  55.8 6.9 %copy-start.6 = (s32[4]{0:T(128)S(1)}, s32[4]{0:T(128)}, u32[]{:S(2)}) copy-start(s32[4]{0:T(128)} %param.19) | copy-start | bytes 52
  55.8 7.0 %copy-start.3 = (bf16[4,512,512]{2,1,0:T(8,128)(2,1)S(1)}, bf16[4,512,512]{2,1,0:T(8,128)(2,1)}, u32[]{:S(2)}) copy-start(bf16[4,512,512]{2,1,0:T(8,128)(2,1)} %param.17) | copy-start | bytes 6291460
  55.8 32.2 %all-to-all-start.1 = ((bf16[128,28,2,128]{3,2,1,0:T(2,128)(2,1)}), bf16[128,28,2,128]{3,2,1,0:T(2,128)(2,1)}, u32[]{:S(2)}, u32[]{:S(2)}) async-start(bf16[128,28,2,128]{3,2,1,0:T(2,128)(2,1)} %bitcast.19), calls=%async_computation.1 | async-start | bytes 3670016 | tf_op jit(solution)/shard_map/all_to_all | solution.py:250
  62.7 1.0 %copy-start.4 = (bf16[4,64,512]{2,1,0:T(8,128)(2,1)S(1)}, bf16[4,64,512]{2,1,0:T(8,128)(2,1)}, u32[]{:S(2)}) copy-start(bf16[4,64,512]{2,1,0:T(8,128)(2,1)} %param.18) | copy-start | bytes 786436
  62.7 0.9 %copy-start.5 = (bf16[4,64,128]{2,1,0:T(8,128)(2,1)S(1)}, bf16[4,64,128]{2,1,0:T(8,128)(2,1)}, u32[]{:S(2)}) copy-start(bf16[4,64,128]{2,1,0:T(8,128)(2,1)} %param.16) | copy-start | bytes 196612
  64.4 23.7 %copy-start.1 = (s32[16,8]{0,1:T(8,128)S(1)}, s32[16,8]{0,1:T(8,128)}, u32[]{:S(2)}) copy-start(s32[16,8]{0,1:T(8,128)} %param.11) | copy-start | bytes 1540
  64.4 23.7 %copy-start.2 = (f32[16,8]{0,1:T(8,128)S(1)}, f32[16,8]{0,1:T(8,128)}, u32[]{:S(2)}) copy-start(f32[16,8]{0,1:T(8,128)} %param.12) | copy-start | bytes 1540

commit v3 on v2

--- a/solution.py
+++ b/solution.py
@@ -121,16 +121,14 @@
     chunk_ref,
     up_hbm,
     down_hbm,
-    out_hbm,
+    out_ref,
     load_ref,
     up_ref,
     down_ref,
     rows_ref,
     act_ref,
     made_ref,
-    out_ref,
     weight_sem,
-    out_sem,
 ):
     ups, downs = up_ref.shape[0], down_ref.shape[0]
     up_width, down_width = up_ref.shape[2], down_ref.shape[2]
@@ -170,35 +168,10 @@
             act_ref[...], down_ref[c], preferred_element_type=F32
         )
 
-    blocks = made_ref.shape[1] // LANES
-    span = 4 * 16 * blocks
-    leave = [
-        pltpu.make_async_copy(
-            out_ref.at[pl.ds(n * span, span), :], out_hbm.at[pl.ds(n * span, span), :], out_sem.at[n]
-        )
-        for n in range(out_ref.shape[0] // span)
-    ]
-
-    def after(group):
-        if group % 4 == 3:
-            leave[group // 4].start()
-
-    rows_to_chunks(made_ref, out_ref, blocks, after)
-    for copy in leave:
-        copy.wait()
-
-
-def combine_kernel(ids_ref, weights_ref, chunk_hbm, out_ref, chunk_ref, rows_ref, sem):
-    blocks = rows_ref.shape[1] // LANES
-    span = 4 * 16 * blocks
-    enter = [
-        pltpu.make_async_copy(
-            chunk_hbm.at[pl.ds(n * span, span), :], chunk_ref.at[pl.ds(n * span, span), :], sem.at[n]
-        )
-        for n in range(chunk_ref.shape[0] // span)
-    ]
-    for copy in enter:
-        copy.start()
+    rows_to_chunks(made_ref, out_ref, made_ref.shape[1] // LANES)
+
+
+def mixer_kernel(ids_ref, weights_ref, after_ref, mixer_ref):
     ids, weights = jnp.transpose(ids_ref[...].astype(F32)), jnp.transpose(weights_ref[...])
     count = ids.shape[1]
     ids = rank_of(ids)
@@ -210,14 +183,30 @@
         return jnp.concatenate([high, value - high], axis=0)
 
     mixer = interleave(parts(jnp.where(slot == 0.0, weight, 0.0)), parts(jnp.where(slot == 1.0, weight, 0.0)))
+    mixer_ref[...] = mixer.astype(BF16)
+
+
+def combine_kernel(mixer_ref, chunk_hbm, out_ref, chunk_ref, rows_ref, sem):
+    blocks = rows_ref.shape[1] // LANES
+    pieces = sem.shape[0]
+    span = chunk_ref.shape[0] // pieces
+    enter = [
+        pltpu.make_async_copy(
+            chunk_hbm.at[pl.ds(n * span, span), :], chunk_ref.at[pl.ds(n * span, span), :], sem.at[n]
+        )
+        for n in range(pieces)
+    ]
+    for copy in enter:
+        copy.start()
+    groups = chunk_ref.shape[0] // (16 * blocks) // pieces
 
     def before(group):
-        if group % 4 == 0:
-            enter[group // 4].wait()
+        if group % groups == 0:
+            enter[group // groups].wait()
 
     chunks_to_rows(chunk_ref, rows_ref, blocks, before)
-    mixed = jnp.dot(mixer.astype(BF16), rows_ref[...], preferred_element_type=F32)
-    rows = ids.shape[0]
+    mixed = jnp.dot(mixer_ref[...], rows_ref[...], preferred_element_type=F32)
+    rows = out_ref.shape[0]
     out_ref[...] = (mixed[:rows] + mixed[rows:]).astype(BF16)
 
 
@@ -281,12 +270,12 @@
             pltpu.VMEM((slots, sent * LANES), F32),
             pltpu.SemaphoreType.DMA((2,)),
         ],
-        compiler_params=pltpu.CompilerParams(vmem_limit_bytes=65_110_016),
+        compiler_params=pltpu.CompilerParams(vmem_limit_bytes=16 << 20),
         name="dispatch",
     )(expert_ids.T, hidden)
     received = exchange(outgoing, experts)
 
-    up_width, down_width = 256, 512
+    up_width, down_width = 256, 1792
     ups, downs = 2 * units // up_width, model_width // down_width
     returned, load = pl.pallas_call(
         expert_kernel,
@@ -295,26 +284,33 @@
             jax.ShapeDtypeStruct((1, experts), F32),
         ),
         in_specs=vmem(1) + hbm(2),
-        out_specs=tuple(hbm(1) + vmem(1)),
+        out_specs=tuple(vmem(2)),
         scratch_shapes=[
             pltpu.VMEM((ups, model_width, up_width), BF16),
             pltpu.VMEM((downs, units, down_width), BF16),
             pltpu.VMEM((slots, sent * LANES), BF16),
             pltpu.VMEM((slots, units), BF16),
             pltpu.VMEM((slots, model_width), F32),
-            pltpu.VMEM((slots * blocks, LANES), BF16),
             pltpu.SemaphoreType.DMA((ups + downs,)),
-            pltpu.SemaphoreType.DMA((4,)),
         ],
-        compiler_params=pltpu.CompilerParams(vmem_limit_bytes=60 * 1024 * 1024),
+        compiler_params=pltpu.CompilerParams(vmem_limit_bytes=48 << 20),
         name="experts",
     )(received, w_gate_up, w_down)
     collected = exchange(returned, experts)
 
+    mixer = pl.pallas_call(
+        mixer_kernel,
+        out_shape=jax.ShapeDtypeStruct((2 * hidden.shape[0], slots), BF16),
+        in_specs=vmem(3),
+        out_specs=pl.BlockSpec(memory_space=pltpu.VMEM),
+        compiler_params=pltpu.CompilerParams(vmem_limit_bytes=4 << 20),
+        name="mixer",
+    )(expert_ids.T, route_weights.T, load)
+
     moe_out = pl.pallas_call(
         combine_kernel,
         out_shape=jax.ShapeDtypeStruct(hidden.shape, BF16),
-        in_specs=vmem(2) + hbm(1),
+        in_specs=vmem(1) + hbm(1),
         out_specs=pl.BlockSpec(memory_space=pltpu.VMEM),
         scratch_shapes=[
             pltpu.VMEM((slots * blocks, LANES), BF16),
@@ -323,7 +319,7 @@
         ],
         compiler_params=pltpu.CompilerParams(vmem_limit_bytes=16 << 20),
         name="combine",
-    )(expert_ids.T, route_weights.T, collected)
+    )(mixer, collected)
     attention_out = attend(query_latent, query_rope, latent_cache, rope_cache, cache_lengths)
     return (moe_out, load[0], attention_out)
 

time: 91.6 us -> 89.1 us (0.973)
  Pallas kernels: 20.4 us -> 15.7 us
  local copies, waits for them, and re-layouts: 0.09 us -> 3.04 us
  matrix products: 4.61 us -> 3.02 us
  waiting for transfers between devices: 20.2 us -> 21.4 us
    pallas_call x1, Pallas kernels: 13.4 us -> 10.3 us  [per_device(): pl.pallas_call(expert_kernel, out_shape=(jax.ShapeDtypeStruct((slots * bl...]
    unnamed x14 -> x22, local copies, waits for them, and re-layouts: 0.09 us -> 3.04 us
    pallas_call x1, Pallas kernels: 3.73 us -> 1.86 us  [per_device(): pl.pallas_call(dispatch_kernel, out_shape=jax.ShapeDtypeStruct((slots * s...]
    dot_general x1, matrix products: 3.45 us -> 1.86 us  [attend(): jnp.einsum('rht,rtc->rhc', attention_weights, latent_cache, preferred_ele...]
    all_to_all x1, waiting for transfers between devices: 20.2 us -> 21.4 us  [exchange(): lax.all_to_all(shaped, AXES, split_axis=0, concat_axis=0, tiled=True)]
  transfers between devices with their start and end apart: 1 -> 1, of which waited for: 1 -> 1; matrix products, arithmetic and copies ran while one was open for 5% -> 4% of each run, Pallas kernels for 0% -> 0%
where the time goes in v3:
time: 89.1 us; the launch traced here: 88.8 us
  blocking collectives  37.7 us (42%)
  waiting for transfers between devices  21.4 us (24%)
  Pallas kernels  15.7 us (18%)
  starting transfers between devices  6.87 us (8%)
  local copies, waits for them, and re-layouts  3.04 us (3%)
  matrix products  3.02 us (3%)
    all_to_all x1, blocking collectives, exchange(): lax.all_to_all(shaped, AXES, split_axis=0, concat_axis=0, tiled=True)  37.7 us
    all_to_all x1, waiting for transfers between devices, exchange(): lax.all_to_all(shaped, AXES, split_axis=0, concat_axis=0, tiled=True)  21.4 us
    pallas_call x1, Pallas kernels, per_device(): pl.pallas_call(expert_kernel, out_shape=(jax.ShapeDtypeStruct((slots * bl...  10.3 us
    all_to_all x1, starting transfers between devices, exchange(): lax.all_to_all(shaped, AXES, split_axis=0, concat_axis=0, tiled=True)  6.87 us
    pallas_call x1, Pallas kernels, per_device(): pl.pallas_call(combine_kernel, out_shape=jax.ShapeDtypeStruct(hidden.shap...  3.13 us
    unnamed x22, local copies, waits for them, and re-layouts  3.04 us
    dot_general x1, matrix products, attend(): jnp.einsum('rht,rtc->rhc', attention_weights, latent_cache, preferred_ele...  1.86 us
    pallas_call x1, Pallas kernels, per_device(): pl.pallas_call(dispatch_kernel, out_shape=jax.ShapeDtypeStruct((slots * s...  1.86 us
  transfers between devices with their start and end apart: 1, of which 1 were waited for; matrix products, arithmetic and copies ran while one was open for 4% of the time, Pallas kernels for 0%

profile of v3, /device:TPU:1, one launch (start us, length us, event | category | flops | bytes accessed | tf_op | source)
XLA Modules:
  0.0 88.8 jit_solution(7270145905690905911)
XLA Ops:
  0.6 0.0 copy-start
  0.6 0.0 copy-start.2
  0.7 1.0 %copy-done.2 = bf16[16,3584]{1,0:T(8,128)(2,1)S(1)} copy-done((bf16[16,3584]{1,0:T(8,128)(2,1)S(1)}, bf16[16,3584]{1,0:T(8,128)(2,1)}, u32[]{:S(2)}) %copy-start.2) | copy-done | bytes 114712
  1.7 0.0 copy-start.3
  1.7 0.7 copy-done.3
  2.4 1.9 %dispatch.1 = bf16[7424,128]{1,0:T(8,128)(2,1)S(1)} custom-call(s32[8,16]{1,0:T(8,128)S(1)} %bitcast.17, bf16[16,3584]{1,0:T(8,128)(2,1)S(1)} %copy-done.2), custom_call_target="tpu_custom_call" | custom-call | tf_op jit(solution)/shard_map/dispatch/pallas_call | solution.py:262
  4.2 37.7 %all_to_all.10 = bf16[128,29,2,128]{3,2,1,0:T(2,128)(2,1)S(1)} all-to-all(bf16[128,29,2,128]{3,2,1,0:T(2,128)(2,1)S(1)} %bitcast.14), channel_id=1, replica_groups=mesh['y'=4,'z'=4,'x'=4,'core'=2] {'core','y','x','z'}, dimensions={0} | all-to-all | bytes 3801088 | tf_op jit(solution)/shard_map/all_to_all | solution.py:239
  41.9 10.3 %experts.1 = (bf16[7168,128]{1,0:T(8,128)(2,1)S(1)}, f32[1,128]{1,0:T(1,128)}) custom-call(bf16[7424,128]{1,0:T(8,128)(2,1)S(1)} %bitcast.15, bf16[1,3584,2048]{2,1,0:T(8,128)(2,1)} %up_hbm.1, bf16[1,1024,3584]{2,1,0:T(8,128)(2,1)} %down_hbm.1), custom_call_target="tpu_custom_call" | custom-call | tf_op jit(solution)/shard_map/experts/pallas_call | solution.py:280
  52.3 0.0 copy-start.1
  52.3 1.2 %copy-done.1 = bf16[7168,128]{1,0:T(8,128)(2,1)} copy-done((bf16[7168,128]{1,0:T(8,128)(2,1)}, bf16[7168,128]{1,0:T(8,128)(2,1)S(1)}, u32[]{:S(2)}) %copy-start.1) | copy-done | bytes 1835032
  53.5 0.0 copy-start.10
  53.5 0.0 copy-start.7
  53.5 6.9 %all-to-all-start.1 = ((bf16[128,28,2,128]{3,2,1,0:T(2,128)(2,1)}), bf16[128,28,2,128]{3,2,1,0:T(2,128)(2,1)}, u32[]{:S(2)}, u32[]{:S(2)}) async-start(bf16[128,28,2,128]{3,2,1,0:T(2,128)(2,1)} %bitcast.16), calls=%async_computation.1 | async-start | bytes 3670016 | tf_op jit(solution)/shard_map/all_to_all | solution.py:239
  60.4 0.0 copy-done.10
  60.4 0.0 copy-start.8
  60.4 0.0 copy-start.9
  60.4 0.1 iota_compare_fusion
  60.5 0.0 copy-done
  60.5 0.0 copy-done.7
  60.5 0.8 fusion.8
  61.3 0.0 copy-done.8
  61.3 0.0 copy-done.9
  61.3 0.4 fusion.4
  61.7 0.3 fusion.7
  62.0 0.0 copy-start.4
  62.0 0.0 copy-start.5
  62.0 0.0 copy-start.6
  62.0 1.9 %convolution_convert_fusion = bf16[4,128,512]{2,1,0:T(8,128)(2,1)} fusion(bf16[4,512,512]{2,1,0:T(8,128)(2,1)S(1)} %copy-done, f32[4,128]{1,0:T(4,128)S(1)} %fusion.7, f32[4,128,512]{2,1,0:T(8,128)S(1)} %fusion.4), kind=kOutput, calls=%fused_computation.6 | convolution fusion | flops 269485056 | bytes 3672064 | tf_op jit(solution)/shard_map/rht,rtc->rhc/dot_general | solution.py:224
  63.9 0.0 copy-done.4
  63.9 0.0 copy-done.5
  63.9 0.0 copy-done.6
  63.9 0.4 mixer.1.mixer_ref
  64.3 21.4 %all-to-all-done.1 = bf16[128,28,2,128]{3,2,1,0:T(2,128)(2,1)} async-done(((bf16[128,28,2,128]{3,2,1,0:T(2,128)(2,1)}), bf16[128,28,2,128]{3,2,1,0:T(2,128)(2,1)}, u32[]{:S(2)}, u32[]{:S(2)}) %all-to-all-start.1) | async-done | bytes 1835040 | tf_op jit(solution)/shard_map/all_to_all | solution.py:239
  85.7 3.1 %combine.1 = bf16[16,3584]{1,0:T(8,128)(2,1)} custom-call(bf16[32,256]{1,0:T(8,128)(2,1)S(1)} %mixer.1.mixer_ref, bf16[7168,128]{1,0:T(8,128)(2,1)} %bitcast.5.chunk_hbm), custom_call_target="tpu_custom_call" | custom-call | tf_op jit(solution)/shard_map/combine/pallas_call | solution.py:310
Async XLA Ops:
  0.6 59.9 %copy-start = (bf16[4,512,512]{2,1,0:T(8,128)(2,1)S(1)}, bf16[4,512,512]{2,1,0:T(8,128)(2,1)}, u32[]{:S(2)}) copy-start(bf16[4,512,512]{2,1,0:T(8,128)(2,1)} %param.17) | copy-start | bytes 6291460
  0.6 1.0 %copy-start.2 = (bf16[16,3584]{1,0:T(8,128)(2,1)S(1)}, bf16[16,3584]{1,0:T(8,128)(2,1)}, u32[]{:S(2)}) copy-start(bf16[16,3584]{1,0:T(8,128)(2,1)} %hidden_hbm.1) | copy-start | bytes 344068
  1.7 0.7 copy-start.3
  52.3 1.2 %copy-start.1 = (bf16[7168,128]{1,0:T(8,128)(2,1)}, bf16[7168,128]{1,0:T(8,128)(2,1)S(1)}, u32[]{:S(2)}) copy-start(bf16[7168,128]{1,0:T(8,128)(2,1)S(1)} %get-tuple-element.6) | copy-start | bytes 5505028
  53.5 6.9 %copy-start.10 = (s32[4]{0:T(128)S(1)}, s32[4]{0:T(128)}, u32[]{:S(2)}) copy-start(s32[4]{0:T(128)} %param.19) | copy-start | bytes 52
  53.5 7.0 %copy-start.7 = (bf16[4,128,512]{2,1,0:T(8,128)(2,1)S(1)}, bf16[4,128,512]{2,1,0:T(8,128)(2,1)}, u32[]{:S(2)}) copy-start(bf16[4,128,512]{2,1,0:T(8,128)(2,1)} %param.15) | copy-start | bytes 1572868
  53.5 32.2 %all-to-all-start.1 = ((bf16[128,28,2,128]{3,2,1,0:T(2,128)(2,1)}), bf16[128,28,2,128]{3,2,1,0:T(2,128)(2,1)}, u32[]{:S(2)}, u32[]{:S(2)}) async-start(bf16[128,28,2,128]{3,2,1,0:T(2,128)(2,1)} %bitcast.16), calls=%async_computation.1 | async-start | bytes 3670016 | tf_op jit(solution)/shard_map/all_to_all | solution.py:239
  60.4 1.0 %copy-start.8 = (bf16[4,64,512]{2,1,0:T(8,128)(2,1)S(1)}, bf16[4,64,512]{2,1,0:T(8,128)(2,1)}, u32[]{:S(2)}) copy-start(bf16[4,64,512]{2,1,0:T(8,128)(2,1)} %param.18) | copy-start | bytes 786436
  60.4 0.9 %copy-start.9 = (bf16[4,64,128]{2,1,0:T(8,128)(2,1)S(1)}, bf16[4,64,128]{2,1,0:T(8,128)(2,1)}, u32[]{:S(2)}) copy-start(bf16[4,64,128]{2,1,0:T(8,128)(2,1)} %param.16) | copy-start | bytes 196612
  62.0 1.9 %copy-start.4 = (s32[16,8]{0,1:T(8,128)S(1)}, s32[16,8]{0,1:T(8,128)}, u32[]{:S(2)}) copy-start(s32[16,8]{0,1:T(8,128)} %param.11) | copy-start | bytes 1540
  62.0 1.9 %copy-start.5 = (f32[16,8]{0,1:T(8,128)S(1)}, f32[16,8]{0,1:T(8,128)}, u32[]{:S(2)}) copy-start(f32[16,8]{0,1:T(8,128)} %param.12) | copy-start | bytes 1540
  62.0 1.9 %copy-start.6 = (f32[1,128]{1,0:T(1,128)S(1)}, f32[1,128]{1,0:T(1,128)}, u32[]{:S(2)}) copy-start(f32[1,128]{1,0:T(1,128)} %get-tuple-element.5.after_ref) | copy-start | bytes 1540
